TPU v7x, 128 devices: a whole 4x4x4 slice. The times are simulated.
128 devices in a mesh: dish: 16 (over y, z_hi, core), chan: 8 (over z_lo, x).
Axes of the slice: x: 4, y: 4, z: 4 (z_hi: 2, z_lo: 2; z = z_hi * 2 + z_lo), core: 2. Of those that a mesh axis runs over, the one named last changes fastest.
Arguments:
- samples: bfloat16 [1024, 1024, 1024], P('chan', 'dish'), may hold values from -6 to 6
- delays: float32 [512, 1024], replicated, may hold values from -32 to 32
- loading: float32 [128], replicated, may hold values from 0.05 to 0.5
- chan_index: int32 [128], replicated, may hold values from 1 to 511, as said below
- dish_map: int32 [1024], replicated, may hold values from 0 to 1023, as said below
- steer_index: int32 [128], replicated, may hold values from 0 to 511
Outputs:
- beams: float32 [128, 2, 1024, 128], P('dish', None, 'chan')
Inputs may be any that keep to these rules, and one draw needn't show every extreme that they name: `chan_index`: 128 distinct channel numbers; 1 and 511 are among them. `dish_map`: each of the 1024 dishes once.
All inputs are finite; a program needn't handle non-finite values.
Results may differ from a plain program's by a relative error of at most 0.017.
Values may be sent and summed in bfloat16 or wider, within the bound.
No kernel may reach another device: no remote copies, remote signals or barrier semaphores. Data moves between devices by JAX's collectives and lax.ppermute only.
A program may use at most 128 MiB of HBM per device.

v0:
```python
import math

import jax
import jax.numpy as jnp
from jax import lax
from jax.sharding import PartitionSpec as P

ITERS = 4


def build_table(chan_index, sample_count):
    positions = jnp.arange(sample_count, dtype=jnp.int32)
    product = positions[:, None] * chan_index[None, :] % sample_count
    angle = product.astype(jnp.float32) * (2.0 * math.pi / sample_count)
    scaling = 1.0 / math.sqrt(sample_count)
    table = jnp.concatenate([jnp.cos(angle) * scaling, -jnp.sin(angle) * scaling], axis=1)
    return table.astype(jnp.bfloat16)


def solve_channel(real_part, imag_part, bin_number, delta, delay_rows, sample_count):
    dish_total = real_part.shape[1]
    beam_count = delay_rows.shape[1]
    stacked = jnp.concatenate([real_part, imag_part], axis=0)
    rotated = jnp.concatenate([imag_part, -real_part], axis=0)
    contract = (((0,), (0,)), ((), ()))
    cov_real = lax.dot_general(stacked, stacked, contract, preferred_element_type=jnp.float32)
    cov_imag = lax.dot_general(rotated, stacked, contract, preferred_element_type=jnp.float32)
    scale_mean = jnp.trace(cov_real) / dish_total + 1e-06
    frobenius = jnp.sum(cov_real * cov_real) + jnp.sum(cov_imag * cov_imag)
    upper = delta + jnp.sqrt(dish_total + frobenius / (scale_mean * scale_mean))
    center = 0.5 * (upper + delta)
    half_width = 0.5 * (upper - delta)
    sigma = center / half_width
    packed_real = cov_real.astype(jnp.bfloat16)
    packed_imag = cov_imag.astype(jnp.bfloat16)
    phase = bin_number.astype(jnp.float32) * delay_rows * (-2.0 * math.pi / sample_count)
    steer_real = jnp.cos(phase)
    steer_imag = jnp.sin(phase)
    solution_real = jnp.zeros_like(steer_real)
    solution_imag = jnp.zeros_like(steer_imag)
    residual_real = steer_real
    residual_imag = steer_imag
    ratio_now = 1.0 / sigma
    direction_real = steer_real / center
    direction_imag = steer_imag / center
    for step in range(ITERS):
        solution_real = solution_real + direction_real
        solution_imag = solution_imag + direction_imag
        packed = jnp.concatenate([direction_real, direction_imag], axis=1).astype(jnp.bfloat16)
        first = jnp.dot(packed_real, packed, preferred_element_type=jnp.float32)
        second = jnp.dot(packed_imag, packed, preferred_element_type=jnp.float32)
        out_real = (
            first[:, :beam_count] - second[:, beam_count:]
        ) / scale_mean + delta * direction_real
        out_imag = (
            second[:, :beam_count] + first[:, beam_count:]
        ) / scale_mean + delta * direction_imag
        residual_real = residual_real - out_real
        residual_imag = residual_imag - out_imag
        if step + 1 < ITERS:
            ratio_next = 1.0 / (2.0 * sigma - ratio_now)
            direction_real = (
                ratio_next * ratio_now * direction_real
                + 2.0 * ratio_next / half_width * residual_real
            )
            direction_imag = (
                ratio_next * ratio_now * direction_imag
                + 2.0 * ratio_next / half_width * residual_imag
            )
            ratio_now = ratio_next
    power = jnp.mean(solution_real * solution_real + solution_imag * solution_imag, axis=0) + 1e-06
    factor = lax.rsqrt(power * dish_total)
    return (
        (solution_real * factor).astype(jnp.bfloat16),
        (solution_imag * factor).astype(jnp.bfloat16),
    )


def flip_parts(values, blocks, inner):
    leading = values.shape[:-1]
    parted = values.reshape(leading + (blocks, 2, inner))
    flipped = jnp.concatenate([parted[..., 1:2, :], -parted[..., 0:1, :]], axis=-2)
    return flipped.reshape(values.shape)


def local(samples, delays, loading, chan_index, dish_map, steer_index):
    frames_local, dish_local, sample_count = samples.shape
    selected = chan_index.shape[0]
    dish_count = lax.axis_size("dish")
    chan_count = lax.axis_size("chan")
    dish_total = dish_local * dish_count
    beam_count = steer_index.shape[0]
    owned = selected // (dish_count * chan_count)
    table = build_table(chan_index, sample_count).reshape(sample_count, 2, selected)
    spectra = jnp.einsum("fjn,nqc->cfqj", samples, table, preferred_element_type=jnp.float32)
    spectra = spectra.astype(jnp.bfloat16).reshape(selected, frames_local, 2 * dish_local)
    received = lax.all_to_all(
        lax.all_to_all(spectra, "dish", split_axis=0, concat_axis=2, tiled=True),
        "chan",
        split_axis=0,
        concat_axis=1,
        tiled=True,
    )
    frames = received.shape[1]
    layered = received.reshape(owned, frames, dish_count, 2, dish_local)
    real_parts = layered[:, :, :, 0, :].reshape(owned, frames, dish_total)
    imag_parts = layered[:, :, :, 1, :].reshape(owned, frames, dish_total)
    first_channel = (lax.axis_index("dish") * chan_count + lax.axis_index("chan")) * owned
    bins = lax.dynamic_slice_in_dim(chan_index, first_channel, owned, 0)
    loads = lax.dynamic_slice_in_dim(loading, first_channel, owned, 0)
    delay_rows = jnp.take(jnp.take(delays, steer_index, axis=0), dish_map, axis=1).T

    def per_channel(items):
        real_part, imag_part, bin_number, delta = items
        weight_real, weight_imag = solve_channel(
            real_part, imag_part, bin_number, delta, delay_rows, sample_count
        )
        arranged = jnp.stack(
            [
                weight_real.reshape(dish_count, dish_local, beam_count),
                weight_imag.reshape(dish_count, dish_local, beam_count),
            ],
            axis=1,
        )
        return arranged.reshape(2 * dish_total, beam_count)

    weights = lax.map(per_channel, (real_parts, imag_parts, bins, loads))
    grouped = lax.all_gather(weights, "chan", axis=0, tiled=True)
    mine = lax.all_to_all(grouped, "dish", split_axis=1, concat_axis=0, tiled=True)
    spectra_flip = flip_parts(spectra, 1, dish_local)
    real_beam = jnp.einsum("cfk,ckb->cfb", spectra, mine, preferred_element_type=jnp.float32)
    imag_beam = jnp.einsum("cfk,ckb->cfb", spectra_flip, mine, preferred_element_type=jnp.float32)
    return lax.psum_scatter(
        jnp.stack([real_beam, imag_beam], axis=1).astype(jnp.bfloat16),
        "dish",
        scatter_dimension=0,
        tiled=True,
    ).astype(jnp.float32)


def solution(mesh):
    return jax.shard_map(
        local,
        mesh=mesh,
        in_specs=(P("chan", "dish", None), P(), P(), P(), P(), P()),
        out_specs=P("dish", None, "chan", None),
        check_vma=False,
    )
```

profile of v0, /device:TPU:0, one launch (start us, length us, event | category | flops | bytes accessed | tf_op | source)
XLA Modules:
  0.0 519.0 jit_solution(1936626272668955001)
XLA Ops:
  6.5 3.3 multiply_convert_fusion.3
  9.8 30.3 %fusion.10 = bf16[2,128,128,64]{2,1,3,0:T(8,128)(2,1)} fusion(bf16[128,64,1024]{2,1,0:T(8,128)(2,1)} %param.6, bf16[1024,1,128]{0,2,1:T(8,128)(2,1)S(1)} %get-tuple-element.48, bf16[1024,1,128]{0,2,1:T(8,128)(2,1)S(1)} %get-tuple-element.47), kind=kOutput, calls=%fused_computation.22 | convolution fusion | flops 4298113024 | bytes 21495808 | tf_op jit(solution)/shard_map/fjn,nqc->cfqj/dot_general | solution.py:95
  40.2 6.9 %copy.42 = bf16[128,128,128]{2,1,0:T(8,128)(2,1)} copy(bf16[128,128,128]{1,0,2:T(8,128)(2,1)} %bitcast.67) | data formatting | bytes 8388608 | tf_op jit(solution)/shard_map/reshape | solution.py:96
  47.1 59.7 %all_to_all.45 = bf16[128,128,128]{2,1,0:T(8,128)(2,1)} all-to-all(bf16[128,128,128]{2,1,0:T(8,128)(2,1)} %copy.42), channel_id=1, replica_groups=mesh['dish'=16,'chan'=8] {'dish'}, dimensions={0} | all-to-all | bytes 8388608 | tf_op jit(solution)/shard_map/all_to_all | solution.py:98
  106.8 6.4 %copy.35 = bf16[8,128,16,128]{1,3,2,0:T(8,128)(2,1)} copy(bf16[8,128,16,128]{3,1,0,2:T(8,128)(2,1)} %bitcast.70) | data formatting | bytes 8388608 | tf_op jit(solution)/shard_map/all_to_all | solution.py:98
  113.3 4.9 all-to-all-start.1
  121.3 2.8 gather_fusion.1
  124.2 43.0 %all-to-all-done.1 = bf16[8,128,2048]{1,2,0:T(8,128)(2,1)} async-done(((bf16[8,128,2048]{1,2,0:T(8,128)(2,1)}), bf16[8,128,2048]{1,2,0:T(8,128)(2,1)}, u32[]{:S(2)}, u32[]{:S(2)}) %all-to-all-start.1) | async-done | bytes 4194336 | tf_op jit(solution)/shard_map/all_to_all | solution.py:97
  167.2 6.2 %copy.36 = bf16[8,128,2048]{1,0,2:T(8,128)(2,1)} copy(bf16[8,128,2048]{1,2,0:T(8,128)(2,1)} %all-to-all-done.1) | data formatting | bytes 8388608 | tf_op jit(solution)/shard_map/all_to_all | solution.py:97
  173.3 7.3 %reshape.114 = bf16[1,1024,16,2,64]{1,4,3,2,0:T(8,128)(2,1)} reshape(bf16[8,128,2048]{1,0,2:T(8,128)(2,1)} %copy.36) | data formatting | bytes 8388608 | tf_op jit(solution)/shard_map/reshape | solution.py:105
  180.6 2.8 fusion.84
  183.7 6.6 %select_reduce_fusion = (f32[]{:T(128)}, f32[]{:T(128)}, bf16[1024,1024]{1,0:T(8,128)(2,1)}) fusion(bf16[1024,1024]{0,1:T(8,128)(2,1)S(1)} %bitcast.75, bf16[1024,1024]{0,1:T(8,128)(2,1)S(1)} %bitcast.71), kind=kOutput, calls=%fused_computation.17 | convolution fusion | flops 4309647360 | bytes 6291464 | tf_op jit(solution)/shard_map/while/body/eval_jaxpr/dot_general | solution.py:26
  190.3 6.5 %multiply_reduce_fusion = (f32[]{:T(128)}, bf16[1024,1024]{1,0:T(8,128)(2,1)}) fusion(bf16[1024,1024]{0,1:T(8,128)(2,1)S(1)} %bitcast.76, bf16[1024,1024]{0,1:T(8,128)(2,1)S(1)} %bitcast.72, bf16[1024,1024]{0,1:T(8,128)(2,1)S(1)} %bitcast_negate_fusion), kind=kOutput, calls=%fused_computation.19 | convolution fusion | flops 4314890240 | bytes 8388612 | tf_op jit(solution)/shard_map/while/body/eval_jaxpr/dot_general | solution.py:27
  201.1 2.7 fusion.77
  203.8 2.3 fusion.57
  206.2 2.5 fusion.58
  208.6 3.6 fusion.75
  214.8 5.4 %fusion.48 = (bf16[1024,128]{1,0:T(8,128)(2,1)S(1)}, bf16[1024,128]{1,0:T(8,128)(2,1)S(1)}) fusion(f32[]{:T(128)S(6)} %div.105, f32[]{:T(128)S(6)} %mul.295, f32[1024,128]{1,0:T(8,128)S(1)} %get-tuple-element.32, f32[]{:T(128)S(6)} %div.100, f32[]{:T(128)S(6)} %mul.287, f32[]{:T(128)} %bitcast.6, f32[]{:T(128)S(6)} %add.165, f32[1024,256]{1,0:T(8,128)S(1)} %fusion.55, ...), kind=kLoop, calls=%fused_computation.82 | loop fusion | flops 3801088 | bytes 4195360 | tf_op jit(solution)/shard_map/convert.4
  221.9 1.8 fusion.54
  223.7 5.6 %add_reduce_fusion = (f32[128]{0:T(128)S(1)}, f32[1024,128]{1,0:T(8,128)S(1)}, f32[1024,128]{1,0:T(8,128)S(1)}) fusion(f32[1024,256]{1,0:T(8,128)} %fusion.53, f32[1024,256]{1,0:T(8,128)} %fusion.54, f32[]{:T(128)S(6)} %div.109, f32[]{:T(128)S(6)} %mul.305, f32[1024,128]{1,0:T(8,128)S(1)} %get-tuple-element.32, f32[]{:T(128)} %bitcast.6, f32[]{:T(128)S(6)} %add.165, ...), kind=kLoop, calls=%fused_computation.71 | loop fusion | flops 6946688 | bytes 6817320 | tf_op jit(solution)/shard_map/while/body/eval_jaxpr/reduce_sum | solution.py:71
  230.3 63.7 %all-gather.2.cloned.1.call-done = bf16[8,2048,128]{2,1,0:T(8,128)(2,1)} async-done(((bf16[1,2048,128]{2,1,0:T(8,128)(2,1)}), bf16[8,2048,128]{2,1,0:T(8,128)(2,1)}) %all-gather.2.cloned.1.call-update) | async-done | bytes 4194320 | tf_op jit(solution)/shard_map/all_gather | solution.py:128
  294.0 6.2 %copy.39 = bf16[8,2048,128]{2,0,1:T(8,128)(2,1)} copy(bf16[8,2048,128]{2,1,0:T(8,128)(2,1)} %all-gather.2.cloned.1.call-done) | data formatting | bytes 8388608 | tf_op jit(solution)/shard_map/all_gather | solution.py:128
  300.2 6.7 %all-to-all-start.2 = ((bf16[8,2048,128]{2,0,1:T(8,128)(2,1)}), bf16[8,2048,128]{2,0,1:T(8,128)(2,1)}, u32[]{:S(2)}, u32[]{:S(2)}) async-start(bf16[8,2048,128]{2,0,1:T(8,128)(2,1)} %copy.39), calls=%async_computation.2 | async-start | bytes 8388608 | tf_op jit(solution)/shard_map/all_to_all | solution.py:129
  307.4 2.6 fusion.83
  310.1 2.3 pad_maximum_fusion.2
  312.4 48.1 %all-to-all-done.2 = bf16[8,2048,128]{2,0,1:T(8,128)(2,1)} async-done(((bf16[8,2048,128]{2,0,1:T(8,128)(2,1)}), bf16[8,2048,128]{2,0,1:T(8,128)(2,1)}, u32[]{:S(2)}, u32[]{:S(2)}) %all-to-all-start.2) | async-done | bytes 4194336 | tf_op jit(solution)/shard_map/all_to_all | solution.py:129
  360.5 3.6 copy.41
  366.3 5.4 %convert_bitcast_fusion = bf16[128,1,128,128]{3,2,0,1:T(8,128)(2,1)} fusion(bf16[128,128,128]{2,1,0:T(8,128)(2,1)S(1)} %bitcast.63, bf16[128,128,128]{1,0,2:T(8,128)(2,1)S(1)} %bitcast.66), kind=kOutput, calls=%fused_computation.15 | convolution fusion | flops 538968064 | bytes 12582912 | tf_op jit(solution)/shard_map/cfk,ckb->cfb/dot_general | solution.py:132
  371.7 6.2 %pad_maximum_fusion = bf16[128,2,128,128]{3,2,0,1:T(8,128)(2,1)} fusion(bf16[128,1,128,128]{3,2,0,1:T(8,128)(2,1)} %convert_bitcast_fusion, bf16[128,1,128,128]{3,2,0,1:T(8,128)(2,1)S(1)} %convert_bitcast_fusion.1), kind=kLoop, calls=%fused_computation.6 | loop fusion | flops 4194304 | bytes 16777216 | tf_op jit(solution)/shard_map/stack | solution.py:134
  377.9 10.4 %copy.47 = bf16[128,2,128,128]{3,2,1,0:T(8,128)(2,1)} copy(bf16[128,2,128,128]{3,2,0,1:T(8,128)(2,1)} %pad_maximum_fusion) | data formatting | bytes 16777216
  388.2 13.8 %copy.63 = bf16[16,8,256,128]{3,1,2,0:T(8,128)(2,1)} copy(bf16[16,8,256,128]{3,2,1,0:T(8,128)(2,1)} %bitcast.65) | data formatting | bytes 16777216
  402.1 107.6 %reduce-scatter.5.cloned.1.call-done = bf16[8,32768]{1,0:T(8,128)(2,1)} async-done(((bf16[128,32768]{1,0:T(8,128)(2,1)}), bf16[8,32768]{1,0:T(8,128)(2,1)}) %reduce-scatter.5.cloned.1.call-update) | async-done | bytes 524304
  (49 shorter events, 12.7 us)
Async XLA Ops:
  6.5 113.6 %copy-start = (f32[512,1024]{1,0:T(8,128)S(1)}, f32[512,1024]{1,0:T(8,128)}, u32[]{:S(2)}) copy-start(f32[512,1024]{1,0:T(8,128)} %param.7) | copy-start | bytes 6291460
  113.3 5.0 copy-start.5
  113.3 6.2 %copy-start.6 = (f32[128]{0:T(128)S(1)}, f32[128]{0:T(128)}, u32[]{:S(2)}) copy-start(f32[128]{0:T(128)} %param.8) | copy-start | bytes 1540
  113.3 6.9 %copy-start.7 = (s32[128]{0:T(128)S(1)}, s32[128]{0:T(128)}, u32[]{:S(2)}) copy-start(s32[128]{0:T(128)} %param.11) | copy-start | bytes 1540
  113.3 53.9 %all-to-all-start.1 = ((bf16[8,128,2048]{1,2,0:T(8,128)(2,1)}), bf16[8,128,2048]{1,2,0:T(8,128)(2,1)}, u32[]{:S(2)}, u32[]{:S(2)}) async-start(bf16[8,128,2048]{1,2,0:T(8,128)(2,1)} %bitcast.69), calls=%async_computation.1 | async-start | bytes 8388608 | tf_op jit(solution)/shard_map/all_to_all | solution.py:97
  118.2 3.1 copy-start.4
  118.2 175.9 %all-gather.2.cloned.1.call-start = ((), (), s32[]{:S(2)}) async-start(), calls=%async_computation.4 | async-start | bytes 4718592 | tf_op jit(solution)/shard_map/all_gather | solution.py:128
  206.2 6.1 %copy-start.10 = (bf16[1024,1024]{1,0:T(8,128)(2,1)S(1)}, bf16[1024,1024]{1,0:T(8,128)(2,1)}, u32[]{:S(2)}) copy-start(bf16[1024,1024]{1,0:T(8,128)(2,1)} %get-tuple-element.51) | copy-start | bytes 6291460
  208.6 4.4 copy-start.8
  214.7 5.4 %copy-start.11 = (bf16[1024,1024]{1,0:T(8,128)(2,1)S(1)}, bf16[1024,1024]{1,0:T(8,128)(2,1)}, u32[]{:S(2)}) copy-start(bf16[1024,1024]{1,0:T(8,128)(2,1)} %get-tuple-element.51) | copy-start | bytes 6291460
  214.8 7.1 %copy-start.9 = (bf16[1024,1024]{1,0:T(8,128)(2,1)S(1)}, bf16[1024,1024]{1,0:T(8,128)(2,1)}, u32[]{:S(2)}) copy-start(bf16[1024,1024]{1,0:T(8,128)(2,1)} %get-tuple-element.49) | copy-start | bytes 6291460
  300.2 60.3 %all-to-all-start.2 = ((bf16[8,2048,128]{2,0,1:T(8,128)(2,1)}), bf16[8,2048,128]{2,0,1:T(8,128)(2,1)}, u32[]{:S(2)}, u32[]{:S(2)}) async-start(bf16[8,2048,128]{2,0,1:T(8,128)(2,1)} %copy.39), calls=%async_computation.2 | async-start | bytes 8388608 | tf_op jit(solution)/shard_map/all_to_all | solution.py:129
  307.0 202.7 %reduce-scatter.5.cloned.1.call-start = ((), (), s32[]{:S(2)}) async-start(), calls=%async_computation.5 | async-start | bytes 8912896
  360.5 3.6 copy-start.2
  364.1 2.2 copy-start.3
  402.1 109.8 %copy-start.1 = (f32[512,1024]{1,0:T(8,128)S(1)}, f32[512,1024]{1,0:T(8,128)}, u32[]{:S(2)}) copy-start(f32[512,1024]{1,0:T(8,128)} %param.7) | copy-start | bytes 6291460
Sparse Core Ops, SparseCore 0:
  230.4 63.5 all-gather.1
  402.2 107.3 reduce-scatter.4
where the time goes:
time: 529 us; the launch traced here: 519 us
  waiting for transfers between devices  262 us (50%)
  local copies, waits for them, and re-layouts  71.6 us (14%)
  matrix products  60.8 us (11%)
  blocking collectives  59.7 us (11%)
  other arithmetic  33.3 us (6%)
  between operations  19 us (4%)
  starting transfers between devices  12.1 us (2%)
    unnamed x3, waiting for transfers between devices  108 us
    all_gather x1, waiting for transfers between devices, local(): grouped = lax.all_gather(weights, 'chan', axis=0, tiled=True)  63.7 us
    all_to_all x1, blocking collectives, local(): lax.all_to_all(spectra, 'dish', split_axis=0, concat_axis=2, tiled=True)  59.7 us
    all_to_all x1, waiting for transfers between devices, local(): lax.all_to_all(grouped, 'dish', split_axis=1, concat_axis=0, tiled=True)  48.1 us
    all_to_all x1, waiting for transfers between devices, local(): lax.all_to_all(lax.all_to_all(spectra, 'dish', split_axis=0, concat_axis=...  43 us
    dot_general x1, matrix products, local(): jnp.einsum('fjn,nqc->cfqj', samples, table, preferred_element_type=jnp.fl...  30.3 us
    unnamed x27, local copies, waits for them, and re-layouts  26.2 us
    another operation x4, other arithmetic  15 us
  transfers between devices with their start and end apart: 4, of which 4 were waited for; matrix products, arithmetic and copies ran while one was open for 2% of the time, Pallas kernels for 0%

commit v1 on v0

v1 whole, which is shorter than its diff:
```python
import functools
import math

import jax
import jax.numpy as jnp
from jax import lax
from jax.experimental import pallas as pl
from jax.experimental.pallas import tpu as pltpu
from jax.sharding import PartitionSpec as P

ITERS = 4
LANES = 128
NT = (((1,), (1,)), ((), ()))


def sincos_turns(turns):
    quarter = jnp.round(turns * 4.0)
    angle = (turns - quarter * 0.25) * (2.0 * math.pi)
    square = angle * angle
    sine = angle * (
        1.0
        + square
        * (-1.0 / 6 + square * (1.0 / 120 + square * (-1.0 / 5040 + square * (1.0 / 362880))))
    )
    cosine = 1.0 + square * (
        -0.5
        + square
        * (
            1.0 / 24
            + square * (-1.0 / 720 + square * (1.0 / 40320 + square * (-1.0 / 3628800)))
        )
    )
    phase = quarter.astype(jnp.int32) & 3
    odd = (phase & 1) == 1
    cos_mag = jnp.where(odd, sine, cosine)
    sin_mag = jnp.where(odd, cosine, sine)
    cos_neg = (phase == 1) | (phase == 2)
    sin_neg = phase >= 2
    return jnp.where(cos_neg, -cos_mag, cos_mag), jnp.where(sin_neg, -sin_mag, sin_mag)


def spectra_kernel(chan_ref, samples_ref, out_ref, table_ref, stage_ref):
    selected = chan_ref.shape[1]
    sample_count = samples_ref.shape[3]
    pairs = samples_ref.shape[1]

    @pl.when(pl.program_id(0) == 0)
    def _():
        chan = jnp.broadcast_to(chan_ref[...].astype(jnp.float32), (selected, selected)).T
        position = lax.broadcasted_iota(jnp.int32, (selected, LANES), 1).astype(jnp.float32)
        turns = chan * position * (1.0 / sample_count)
        cosine, sine = sincos_turns(turns - jnp.round(turns))
        scaling = 1.0 / math.sqrt(sample_count)
        cosine = cosine * scaling
        sine = sine * scaling
        jump = chan * (float(LANES) / sample_count)
        jump_cos, jump_sin = sincos_turns(jump - jnp.round(jump))
        for block in range(sample_count // LANES):
            span = slice(block * LANES, (block + 1) * LANES)
            table_ref[0:selected, span] = cosine.astype(jnp.bfloat16)
            table_ref[selected : 2 * selected, span] = (-sine).astype(jnp.bfloat16)
            cosine, sine = (
                cosine * jump_cos - sine * jump_sin,
                sine * jump_cos + cosine * jump_sin,
            )

    table = table_ref[...]
    for pair in range(0, pairs, 2):
        rows = jnp.concatenate(
            [
                samples_ref[0, pair],
                samples_ref[1, pair],
                samples_ref[0, pair + 1],
                samples_ref[1, pair + 1],
            ],
            axis=0,
        )
        values = lax.dot_general(table, rows, NT, preferred_element_type=jnp.float32)
        for extra in range(2):
            for part in range(2):
                stage_ref[pl.ds(part * pairs + pair + extra, selected, stride=2 * pairs), :] = (
                    values[
                        part * selected : (part + 1) * selected,
                        extra * LANES : (extra + 1) * LANES,
                    ]
                )
    out_ref[...] = stage_ref[...].reshape(selected, 2, pairs, LANES).astype(jnp.bfloat16)


def spectra_call(samples, chan_index):
    frames, dishes, sample_count = samples.shape
    selected = chan_index.shape[0]
    half = frames // 2
    pairs = 16
    return pl.pallas_call(
        spectra_kernel,
        out_shape=jax.ShapeDtypeStruct((selected, 2, half, LANES), jnp.bfloat16),
        grid=(half // pairs,),
        in_specs=[
            pl.BlockSpec((1, selected), lambda i: (0, 0)),
            pl.BlockSpec((2, pairs, dishes, sample_count), lambda i: (0, i, 0, 0)),
        ],
        out_specs=pl.BlockSpec((selected, 2, pairs, LANES), lambda i: (0, 0, i, 0)),
        scratch_shapes=[
            pltpu.VMEM((2 * selected, sample_count), jnp.bfloat16),
            pltpu.VMEM((selected * 2 * pairs, LANES), jnp.float32),
        ],
        name="spectra",
    )(chan_index.reshape(1, selected), samples.reshape(2, half, dishes, sample_count))


def solve_kernel(
    sample_count,
    own_ref,
    chan_ref,
    load_ref,
    recv_ref,
    delay_ref,
    out_ref,
    joined_ref,
    turned_ref,
    real_ref,
    imag_ref,
    state_ref,
):
    blocks, groups, _, half, _ = recv_ref.shape
    dish_total, beam_count = delay_ref.shape
    dish_local = dish_total // blocks
    span = groups * half
    frames = 2 * span
    own = own_ref[0]
    delta = load_ref[own]
    bin_number = chan_ref[own].astype(jnp.float32)

    for block in range(blocks):
        rows = slice(block * dish_local, (block + 1) * dish_local)
        for part in range(2):
            piece = recv_ref[block, :, part].reshape(span, LANES)
            flipped = piece.T
            for side in range(2):
                values = flipped[side * dish_local : (side + 1) * dish_local, :]
                first = part * frames + side * span
                joined_ref[rows, first : first + span] = values
                other = (1 - part) * frames + side * span
                turned_ref[rows, other : other + span] = values if part == 1 else -values

    step = 256
    trace = jnp.float32(0.0)
    energy = jnp.float32(0.0)
    for first in range(0, dish_total, step):
        cols = slice(first, first + step)
        right = joined_ref[cols, :]
        cov_real = lax.dot_general(joined_ref[...], right, NT, preferred_element_type=jnp.float32)
        cov_imag = lax.dot_general(turned_ref[...], right, NT, preferred_element_type=jnp.float32)
        diagonal = cov_real[first : first + step, :]
        same = lax.broadcasted_iota(jnp.int32, (step, step), 0) == lax.broadcasted_iota(
            jnp.int32, (step, step), 1
        )
        trace = trace + jnp.sum(jnp.where(same, diagonal, 0.0))
        energy = energy + jnp.sum(cov_real * cov_real + cov_imag * cov_imag)
        real_ref[:, cols] = cov_real.astype(jnp.bfloat16)
        imag_ref[:, cols] = cov_imag.astype(jnp.bfloat16)

    def full(value):
        return jnp.full((1, beam_count), value, jnp.float32)

    scale_mean = full(trace) / dish_total + 1e-06
    load = full(delta)
    upper = load + jnp.sqrt(dish_total + full(energy) / (scale_mean * scale_mean))
    center = 0.5 * (upper + load)
    half_width = 0.5 * (upper - load)
    sigma = center / half_width
    inverse_scale = 1.0 / scale_mean
    inverse_center = 1.0 / center

    turns = bin_number * delay_ref[...] * (-1.0 / sample_count)
    steer_real, steer_imag = sincos_turns(turns - jnp.round(turns))
    sol_real = steer_real * inverse_center
    sol_imag = steer_imag * inverse_center
    res_real, res_imag = steer_real, steer_imag
    dir_real, dir_imag = sol_real, sol_imag
    ratio_now = 1.0 / sigma
    for turn in range(ITERS - 1):
        state_ref[:, 0:beam_count] = dir_real.astype(jnp.bfloat16)
        state_ref[:, beam_count : 2 * beam_count] = dir_imag.astype(jnp.bfloat16)
        packed = state_ref[...]
        first = jnp.dot(real_ref[...], packed, preferred_element_type=jnp.float32)
        second = jnp.dot(imag_ref[...], packed, preferred_element_type=jnp.float32)
        res_real = res_real - (
            (first[:, :beam_count] - second[:, beam_count:]) * inverse_scale + load * dir_real
        )
        res_imag = res_imag - (
            (second[:, :beam_count] + first[:, beam_count:]) * inverse_scale + load * dir_imag
        )
        ratio_next = 1.0 / (2.0 * sigma - ratio_now)
        keep = ratio_next * ratio_now
        gain = 2.0 * ratio_next / half_width
        dir_real = keep * dir_real + gain * res_real
        dir_imag = keep * dir_imag + gain * res_imag
        ratio_now = ratio_next
        sol_real = sol_real + dir_real
        sol_imag = sol_imag + dir_imag

    power = jnp.sum(sol_real * sol_real + sol_imag * sol_imag, axis=0, keepdims=True) / dish_total
    factor = lax.rsqrt((power + 1e-06) * dish_total)
    weight_real = (sol_real * factor).astype(jnp.bfloat16)
    weight_imag = (sol_imag * factor).astype(jnp.bfloat16)

    total = jnp.zeros((span, 4 * beam_count), jnp.float32)
    empty = jnp.zeros((dish_local, 2 * beam_count), jnp.bfloat16)
    for block in range(blocks):
        rows = slice(block * dish_local, (block + 1) * dish_local)
        wr, wi = weight_real[rows, :], weight_imag[rows, :]
        on_real = jnp.concatenate([wr, -wi], axis=1)
        on_imag = jnp.concatenate([wi, wr], axis=1)
        right = jnp.concatenate(
            [
                jnp.concatenate([on_real, empty], axis=1),
                jnp.concatenate([empty, on_real], axis=1),
                jnp.concatenate([on_imag, empty], axis=1),
                jnp.concatenate([empty, on_imag], axis=1),
            ],
            axis=0,
        )
        left = jnp.concatenate(
            [
                recv_ref[block, :, 0].reshape(span, LANES),
                recv_ref[block, :, 1].reshape(span, LANES),
            ],
            axis=1,
        )
        total = total + jnp.dot(left, right, preferred_element_type=jnp.float32)
    for group in range(groups):
        for side in range(2):
            for part in range(2):
                first = (2 * side + part) * beam_count
                out_ref[group, part, side * half : (side + 1) * half, :] = total[
                    group * half : (group + 1) * half, first : first + beam_count
                ].astype(jnp.bfloat16)


def solve_call(sample_count, own, chan_index, loading, received, delay_rows):
    blocks, groups, _, half, _ = received.shape
    dish_total, beam_count = delay_rows.shape
    frames = 2 * groups * half
    smem = pl.BlockSpec(memory_space=pltpu.SMEM)
    vmem = pl.BlockSpec(memory_space=pltpu.VMEM)
    return pl.pallas_call(
        functools.partial(solve_kernel, sample_count),
        out_shape=jax.ShapeDtypeStruct((groups, 2, 2 * half, beam_count), jnp.bfloat16),
        in_specs=[smem, smem, smem, vmem, vmem],
        out_specs=vmem,
        scratch_shapes=[
            pltpu.VMEM((dish_total, 2 * frames), jnp.bfloat16),
            pltpu.VMEM((dish_total, 2 * frames), jnp.bfloat16),
            pltpu.VMEM((dish_total, dish_total), jnp.bfloat16),
            pltpu.VMEM((dish_total, dish_total), jnp.bfloat16),
            pltpu.VMEM((dish_total, 2 * beam_count), jnp.bfloat16),
        ],
        name="solve",
    )(own, chan_index, loading, received, delay_rows)


def local(samples, delays, loading, chan_index, dish_map, steer_index):
    dish_count = lax.axis_size("dish")
    chan_count = lax.axis_size("chan")
    own = (lax.axis_index("dish") * chan_count + lax.axis_index("chan")).reshape(1)
    spectra = spectra_call(samples, chan_index)
    received = lax.all_to_all(spectra, ("dish", "chan"), 0, 0, tiled=True)
    received = received.reshape((dish_count, chan_count) + received.shape[1:])
    delay_rows = jnp.take(jnp.take(delays, steer_index, axis=0), dish_map, axis=1).T
    beams = solve_call(samples.shape[2], own, chan_index, loading, received, delay_rows)
    return lax.all_to_all(beams, "chan", 0, 0, tiled=True).astype(jnp.float32)


def solution(mesh):
    return jax.shard_map(
        local,
        mesh=mesh,
        in_specs=(P("chan", "dish", None), P(), P(), P(), P(), P()),
        out_specs=P("dish", None, "chan", None),
        check_vma=False,
    )
```

time: 529 us -> 113 us (0.21); the launches traced: 519 us -> 113 us
  waiting for transfers between devices: 262 us -> 48.2 us
  local copies, waits for them, and re-layouts: 71.6 us -> 3.82 us
  matrix products: 60.8 us -> 0 us
  blocking collectives: 59.7 us -> 13.4 us
  Pallas kernels: 0 us -> 33.1 us
  other arithmetic: 33.3 us -> 2.2 us
  between operations: 19 us -> 0.12 us
    unnamed x3 -> x0, waiting for transfers between devices: 108 us -> none
    all_gather x1 -> x0, waiting for transfers between devices: 63.7 us -> none  [local(): grouped = lax.all_gather(weights, 'chan', axis=0, tiled=True)]
    dot_general x11 -> x0, matrix products: 60.8 us -> none  [the longest x1 30.3 us: local(): jnp.einsum('fjn,nqc->cfqj', samples, table, preferred_element_type=jnp.fl...]
    all_to_all x1, blocking collectives: 59.7 us -> 13.4 us  [local(): return lax.all_to_all(beams, 'chan', 0, 0, tiled=True).astype(jnp.float32)]
    all_to_all x2 -> x1, waiting for transfers between devices: 91.1 us -> 48.2 us  [local(): received = lax.all_to_all(spectra, ('dish', 'chan'), 0, 0, tiled=True)]
    pallas_call x0 -> x2, Pallas kernels: none -> 33.1 us  [the longest x1 19.2 us: solve_call(): pl.pallas_call(functools.partial(solve_kernel, sample_count), out_shape=j...]
    unnamed x27 -> x6, local copies, waits for them, and re-layouts: 26.2 us -> 0.01 us
    another operation x6 -> x0, other arithmetic: 22.1 us -> none
  transfers between devices with their start and end apart: 4 -> 1, of which waited for: 4 -> 1; matrix products, arithmetic and copies ran while one was open for 2% -> 4% of each run, Pallas kernels for 0% -> 0%
where the time goes in v1:
time: 113 us
  waiting for transfers between devices  48.2 us (43%)
  Pallas kernels  33.1 us (29%)
  blocking collectives  13.4 us (12%)
  starting transfers between devices  11.9 us (11%)
  local copies, waits for them, and re-layouts  3.82 us (3%)
  other arithmetic  2.2 us (2%)
    all_to_all x1, waiting for transfers between devices, local(): received = lax.all_to_all(spectra, ('dish', 'chan'), 0, 0, tiled=True)  48.2 us
    pallas_call x1, Pallas kernels, solve_call(): pl.pallas_call(functools.partial(solve_kernel, sample_count), out_shape=j...  19.2 us
    pallas_call x1, Pallas kernels, spectra_call(): pl.pallas_call(spectra_kernel, out_shape=jax.ShapeDtypeStruct((selected,...  13.8 us
    all_to_all x1, blocking collectives, local(): return lax.all_to_all(beams, 'chan', 0, 0, tiled=True).astype(jnp.float32)  13.4 us
    all_to_all x1, starting transfers between devices, local(): received = lax.all_to_all(spectra, ('dish', 'chan'), 0, 0, tiled=True)  11.9 us
    gather x1, local copies, waits for them, and re-layouts, local(): jnp.take(jnp.take(delays, steer_index, axis=0), dish_map, axis=1)  2.81 us
  transfers between devices with their start and end apart: 1, of which 1 were waited for; matrix products, arithmetic and copies ran while one was open for 4% of the time, Pallas kernels for 0%

profile of v1, /device:TPU:0, one launch (start us, length us, event | category | flops | bytes accessed | tf_op | source)
XLA Modules:
  0.0 112.7 jit_solution(13452252821973477229)
XLA Ops:
  0.0 0.0 copy-start
  0.0 13.8 %spectra.1 = bf16[128,2,64,128]{3,2,1,0:T(8,128)(2,1)} custom-call(s32[1,128]{1,0:T(1,128)} %bitcast.5, bf16[2,64,64,1024]{3,2,1,0:T(8,128)(2,1)} %bitcast.4), custom_call_target="tpu_custom_call" | custom-call | tf_op jit(solution)/shard_map/spectra/pallas_call | solution.py:95
  13.8 0.0 copy-start.2
  13.8 11.9 %all-to-all-start = ((bf16[128,2,64,128]{3,2,1,0:T(8,128)(2,1)}), bf16[128,2,64,128]{3,2,1,0:T(8,128)(2,1)}, u32[]{:S(2)}, u32[]{:S(2)}) async-start(bf16[128,2,64,128]{3,2,1,0:T(8,128)(2,1)} %spectra.1), calls=%async_computation | async-start | bytes 8388608 | tf_op jit(solution)/shard_map/all_to_all | solution.py:269
  25.7 0.0 copy-start.1
  25.8 0.0 copy-done.2
  25.8 0.0 copy-done
  25.8 0.8 gather_fusion
  26.6 0.1 broadcast_select_fusion.1
  26.7 0.2 copy.7
  26.9 0.0 copy-done.1
  27.0 2.8 %gather_fusion.1 = f32[1024,128]{1,0:T(8,128)S(1)} fusion(f32[128,1024]{0,1:T(8,128)S(1)} %copy.7, s32[1024]{0:T(1024)S(1)} %fusion), kind=kCustom, calls=%fused_computation.1 | custom fusion | bytes 1052672 | tf_op jit(solution)/shard_map/jit(_take)/gather | solution.py:271
  29.8 1.0 broadcast_select_fusion.delay_ref
  30.8 48.2 %all-to-all-done = bf16[128,2,64,128]{3,2,1,0:T(8,128)(2,1)} async-done(((bf16[128,2,64,128]{3,2,1,0:T(8,128)(2,1)}), bf16[128,2,64,128]{3,2,1,0:T(8,128)(2,1)}, u32[]{:S(2)}, u32[]{:S(2)}) %all-to-all-start) | async-done | bytes 4194336 | tf_op jit(solution)/shard_map/all_to_all | solution.py:269
  79.0 19.2 %solve.1 = bf16[8,2,128,128]{3,2,1,0:T(8,128)(2,1)} custom-call(s32[1]{0:T(128)} %bitcast.own_ref, s32[128]{0:T(128)} %chan_ref.1, f32[128]{0:T(128)} %load_ref.1, bf16[16,8,2,64,128]{4,3,2,1,0:T(8,128)(2,1)} %bitcast.3.recv_ref, f32[1024,128]{1,0:T(8,128)} %broadcast_select_fusion.delay_ref), custom_call_target="tpu_custom_call" | custom-call | tf_op jit(solution)/shard_map/solve/pallas_call | solution.py:248
  98.2 13.4 %all_to_all.10 = bf16[8,2,128,128]{3,2,1,0:T(8,128)(2,1)S(1)} all-to-all(bf16[8,2,128,128]{3,2,1,0:T(8,128)(2,1)} %solve.1), channel_id=1, replica_groups=mesh['dish'=16,'chan'=8] {'chan'}, dimensions={0} | all-to-all | bytes 1048576 | tf_op jit(solution)/shard_map/all_to_all | solution.py:273
  111.6 1.1 convert_element_type.3
  (5 shorter events, 0.0 us)
Async XLA Ops:
  0.0 25.8 %copy-start = (f32[512,1024]{1,0:T(8,128)S(1)}, f32[512,1024]{1,0:T(8,128)}, u32[]{:S(2)}) copy-start(f32[512,1024]{1,0:T(8,128)} %param.7) | copy-start | bytes 6291460
  13.8 11.9 %copy-start.2 = (s32[128]{0:T(128)S(1)}, s32[128]{0:T(128)}, u32[]{:S(2)}) copy-start(s32[128]{0:T(128)} %param.11) | copy-start | bytes 1540
  13.8 65.1 %all-to-all-start = ((bf16[128,2,64,128]{3,2,1,0:T(8,128)(2,1)}), bf16[128,2,64,128]{3,2,1,0:T(8,128)(2,1)}, u32[]{:S(2)}, u32[]{:S(2)}) async-start(bf16[128,2,64,128]{3,2,1,0:T(8,128)(2,1)} %spectra.1), calls=%async_computation | async-start | bytes 8388608 | tf_op jit(solution)/shard_map/all_to_all | solution.py:269
  25.7 1.2 %copy-start.1 = (s32[1024]{0:T(1024)S(1)}, s32[1024]{0:T(1024)}, u32[]{:S(2)}) copy-start(s32[1024]{0:T(1024)} %param.10) | copy-start | bytes 12292

commit v2 on v1

v2 whole, which is shorter than its diff:
```python
import functools
import math

import jax
import jax.numpy as jnp
from jax import lax
from jax.experimental import pallas as pl
from jax.experimental.pallas import tpu as pltpu
from jax.sharding import PartitionSpec as P

ITERS = 4
PIECES = (16, 16, 16, 16)
WIDE = 2
LANES = 128
TILE = 256
NT = (((1,), (1,)), ((), ()))


def sincos_turns(turns):
    quarter = jnp.round(turns * 4.0)
    angle = (turns - quarter * 0.25) * (2.0 * math.pi)
    square = angle * angle
    sine = angle * (
        1.0
        + square
        * (-1.0 / 6 + square * (1.0 / 120 + square * (-1.0 / 5040 + square * (1.0 / 362880))))
    )
    cosine = 1.0 + square * (
        -0.5
        + square
        * (
            1.0 / 24
            + square * (-1.0 / 720 + square * (1.0 / 40320 + square * (-1.0 / 3628800)))
        )
    )
    phase = quarter.astype(jnp.int32) & 3
    odd = (phase & 1) == 1
    cos_mag = jnp.where(odd, sine, cosine)
    sin_mag = jnp.where(odd, cosine, sine)
    cos_neg = (phase == 1) | (phase == 2)
    sin_neg = phase >= 2
    return jnp.where(cos_neg, -cos_mag, cos_mag), jnp.where(sin_neg, -sin_mag, sin_mag)


def spectra_kernel(
    chan_ref, samples_ref, out_ref, table_ref, held_ref, stage_ref, ready_ref, in_sems, out_sems
):
    selected = chan_ref.shape[1]
    sample_count = samples_ref.shape[3]
    half = samples_ref.shape[1]
    groups = out_sems.shape[0]
    pairs = half // groups

    loads = {}
    first = 0
    for piece, size in enumerate(PIECES):
        rows = slice(first, first + size)
        loads[first] = pltpu.make_async_copy(
            samples_ref.at[:, rows], held_ref.at[:, rows], in_sems.at[piece]
        )
        loads[first].start()
        first += size

    chan = jnp.broadcast_to(chan_ref[...].astype(jnp.float32), (selected, selected)).T
    position = lax.broadcasted_iota(jnp.int32, (selected, LANES), 1).astype(jnp.float32)
    turns = chan * position * (1.0 / sample_count)
    cosine, sine = sincos_turns(turns - jnp.round(turns))
    scaling = 1.0 / math.sqrt(sample_count)
    cosine = cosine * scaling
    sine = sine * scaling
    jump = chan * (float(LANES) / sample_count)
    jump_cos, jump_sin = sincos_turns(jump - jnp.round(jump))
    for block in range(sample_count // LANES):
        span = slice(block * LANES, (block + 1) * LANES)
        table_ref[0:selected, span] = cosine.astype(jnp.bfloat16)
        table_ref[selected : 2 * selected, span] = (-sine).astype(jnp.bfloat16)
        cosine, sine = (
            cosine * jump_cos - sine * jump_sin,
            sine * jump_cos + cosine * jump_sin,
        )

    stores = []
    stride = stage_ref.shape[1] // selected
    for group in range(groups):
        slot = group % 2
        for pair in range(0, pairs, WIDE):
            place = group * pairs + pair
            if place in loads:
                loads[place].wait()
            rows = jnp.concatenate(
                [held_ref[side, place + extra] for extra in range(WIDE) for side in range(2)],
                axis=0,
            )
            values = lax.dot_general(
                table_ref[...], rows, NT, preferred_element_type=jnp.float32
            )
            for extra in range(WIDE):
                for part in range(2):
                    stage_ref[
                        slot, pl.ds(part * pairs + pair + extra, selected, stride=stride), :
                    ] = values[
                        part * selected : (part + 1) * selected,
                        extra * LANES : (extra + 1) * LANES,
                    ]
        rows = slice(group * pairs, (group + 1) * pairs)
        staged = stage_ref[slot].reshape(selected, stride, LANES)[:, : 2 * pairs]
        ready_ref[:, :, rows] = staged.astype(jnp.bfloat16).reshape(selected, 2, pairs, LANES)
        stores.append(
            pltpu.make_async_copy(
                ready_ref.at[:, :, rows], out_ref.at[:, :, rows], out_sems.at[group]
            )
        )
        stores[-1].start()
    for store in stores:
        store.wait()


def spectra_call(samples, chan_index):
    frames, dishes, sample_count = samples.shape
    selected = chan_index.shape[0]
    half = frames // 2
    groups = 4
    stride = 2 * half // groups + 8
    hbm = pl.BlockSpec(memory_space=pl.ANY)
    return pl.pallas_call(
        spectra_kernel,
        out_shape=jax.ShapeDtypeStruct((selected, 2, half, LANES), jnp.bfloat16),
        in_specs=[pl.BlockSpec(memory_space=pltpu.VMEM), hbm],
        out_specs=hbm,
        scratch_shapes=[
            pltpu.VMEM((2 * selected, sample_count), jnp.bfloat16),
            pltpu.VMEM((2, half, dishes, sample_count), jnp.bfloat16),
            pltpu.VMEM((2, selected * stride, LANES), jnp.float32),
            pltpu.VMEM((selected, 2, half, LANES), jnp.bfloat16),
            pltpu.SemaphoreType.DMA((len(PIECES),)),
            pltpu.SemaphoreType.DMA((groups,)),
        ],
        name="spectra",
    )(chan_index.reshape(1, selected), samples.reshape(2, half, dishes, sample_count))


def solve_kernel(
    sample_count,
    own_ref,
    chan_ref,
    load_ref,
    recv_ref,
    delay_ref,
    out_ref,
    held_ref,
    joined_ref,
    turned_ref,
    real_ref,
    imag_ref,
    packed_ref,
    sol_ref,
    res_ref,
    dir_ref,
    weight_ref,
    sems,
):
    blocks, groups, _, half, _ = recv_ref.shape
    dish_total, beam_count = delay_ref.shape
    dish_local = dish_total // blocks
    span = groups * half
    frames = 2 * span
    own = own_ref[0]
    delta = load_ref[own]
    bin_number = chan_ref[own].astype(jnp.float32)
    on_real, on_imag = slice(0, beam_count), slice(beam_count, 2 * beam_count)

    loads = []
    each = blocks // sems.shape[0]
    for index in range(sems.shape[0]):
        part = slice(index * each, (index + 1) * each)
        loads.append(pltpu.make_async_copy(recv_ref.at[part], held_ref.at[part], sems.at[index]))
        loads[-1].start()

    turns = bin_number * delay_ref[...] * (-1.0 / sample_count)
    steer_real, steer_imag = sincos_turns(turns - jnp.round(turns))
    res_ref[:, on_real] = steer_real
    res_ref[:, on_imag] = steer_imag

    for block in range(blocks):
        if block % each == 0:
            loads[block // each].wait()
        rows = slice(block * dish_local, (block + 1) * dish_local)
        for part in range(2):
            flipped = held_ref[block, :, part].reshape(span, LANES).T
            for side in range(2):
                values = flipped[side * dish_local : (side + 1) * dish_local, :]
                first = part * frames + side * span
                joined_ref[rows, first : first + span] = values
                other = (1 - part) * frames + side * span
                turned_ref[rows, other : other + span] = values if part == 1 else -values

    tiles = [slice(first, first + TILE) for first in range(0, dish_total, TILE)]
    same = lax.broadcasted_iota(jnp.int32, (TILE, TILE), 0) == lax.broadcasted_iota(
        jnp.int32, (TILE, TILE), 1
    )
    trace = jnp.zeros((1, TILE), jnp.float32)
    energy = jnp.zeros((1, TILE), jnp.float32)
    for index, cols in enumerate(tiles):
        right = joined_ref[cols, :]
        top = cols.stop
        cov_real = lax.dot_general(
            joined_ref[0:top, :], right, NT, preferred_element_type=jnp.float32
        )
        cov_imag = lax.dot_general(
            turned_ref[0:top, :], right, NT, preferred_element_type=jnp.float32
        )
        square = cov_real * cov_real + cov_imag * cov_imag
        trace = trace + jnp.sum(jnp.where(same, cov_real[cols, :], 0.0), axis=0, keepdims=True)
        energy = energy + jnp.sum(square[cols, :], axis=0, keepdims=True)
        packed_real = cov_real.astype(jnp.bfloat16)
        packed_imag = cov_imag.astype(jnp.bfloat16)
        real_ref[0:top, cols] = packed_real
        imag_ref[0:top, cols] = packed_imag
        if index:
            energy = energy + 2.0 * jnp.sum(square[0 : cols.start, :], axis=0, keepdims=True)
        for rows in tiles[:index]:
            real_ref[cols, rows] = packed_real[rows, :].T
            imag_ref[cols, rows] = -packed_imag[rows, :].T

    def full(value):
        return jnp.full((1, 2 * beam_count), value, jnp.float32)

    scale_mean = full(jnp.sum(trace)) / dish_total + 1e-06
    load = full(delta)
    upper = load + jnp.sqrt(dish_total + full(jnp.sum(energy)) / (scale_mean * scale_mean))
    center = 0.5 * (upper + load)
    half_width = 0.5 * (upper - load)
    sigma = center / half_width
    inverse_scale = (1.0 / scale_mean)[:, on_real]
    inverse_center = 1.0 / center

    ratio_now = 1.0 / sigma
    power = jnp.zeros((1, 2 * beam_count), jnp.float32)
    for rows in tiles:
        first = res_ref[rows, :] * inverse_center
        sol_ref[rows, :] = first
        dir_ref[rows, :] = first
        packed_ref[0, rows, :] = first.astype(jnp.bfloat16)
    for turn in range(ITERS - 1):
        ratio_next = 1.0 / (2.0 * sigma - ratio_now)
        keep = ratio_next * ratio_now
        gain = 2.0 * ratio_next / half_width
        ratio_now = ratio_next
        packed = packed_ref[turn % 2]
        for rows in tiles:
            by_real = jnp.dot(real_ref[rows, :], packed, preferred_element_type=jnp.float32)
            by_imag = jnp.dot(imag_ref[rows, :], packed, preferred_element_type=jnp.float32)
            image = jnp.concatenate(
                [
                    (by_real[:, on_real] - by_imag[:, on_imag]) * inverse_scale,
                    (by_imag[:, on_real] + by_real[:, on_imag]) * inverse_scale,
                ],
                axis=1,
            )
            old = dir_ref[rows, :]
            residual = res_ref[rows, :] - (image + load * old)
            new = keep * old + gain * residual
            total = sol_ref[rows, :] + new
            sol_ref[rows, :] = total
            if turn + 2 < ITERS:
                res_ref[rows, :] = residual
                dir_ref[rows, :] = new
                packed_ref[(turn + 1) % 2, rows, :] = new.astype(jnp.bfloat16)
            else:
                power = power + jnp.sum(total * total, axis=0, keepdims=True)

    power = (power[:, on_real] + power[:, on_imag]) / dish_total
    factor = lax.rsqrt((power + 1e-06) * dish_total)
    for rows in tiles:
        weight_real = (sol_ref[rows, on_real] * factor).astype(jnp.bfloat16).T
        weight_imag = (sol_ref[rows, on_imag] * factor).astype(jnp.bfloat16).T
        weight_ref[0, on_real, rows] = weight_real
        weight_ref[0, on_imag, rows] = -weight_imag
        weight_ref[1, on_real, rows] = weight_imag
        weight_ref[1, on_imag, rows] = weight_real

    for side in range(2):
        for first in range(0, span, TILE):
            place = side * span + first
            beams = jnp.dot(
                weight_ref[0],
                joined_ref[:, place : place + TILE],
                preferred_element_type=jnp.float32,
            ) + jnp.dot(
                weight_ref[1],
                joined_ref[:, frames + place : frames + place + TILE],
                preferred_element_type=jnp.float32,
            )
            beams = beams.astype(jnp.bfloat16)
            for part, lanes in enumerate((on_real, on_imag)):
                flipped = beams[lanes, :].T
                for group in range(TILE // half):
                    out_ref[first // half + group, part, side * half : (side + 1) * half, :] = (
                        flipped[group * half : (group + 1) * half, :]
                    )


def solve_call(sample_count, own, chan_index, loading, received, delay_rows):
    blocks, groups, _, half, _ = received.shape
    dish_total, beam_count = delay_rows.shape
    frames = 2 * groups * half
    smem = pl.BlockSpec(memory_space=pltpu.SMEM)
    vmem = pl.BlockSpec(memory_space=pltpu.VMEM)
    hbm = pl.BlockSpec(memory_space=pl.ANY)
    wide = (dish_total, 2 * beam_count)
    return pl.pallas_call(
        functools.partial(solve_kernel, sample_count),
        out_shape=jax.ShapeDtypeStruct((groups, 2, 2 * half, beam_count), jnp.bfloat16),
        in_specs=[smem, smem, smem, hbm, vmem],
        out_specs=vmem,
        scratch_shapes=[
            pltpu.VMEM(received.shape, jnp.bfloat16),
            pltpu.VMEM((dish_total, 2 * frames), jnp.bfloat16),
            pltpu.VMEM((dish_total, 2 * frames), jnp.bfloat16),
            pltpu.VMEM((dish_total, dish_total), jnp.bfloat16),
            pltpu.VMEM((dish_total, dish_total), jnp.bfloat16),
            pltpu.VMEM((2,) + wide, jnp.bfloat16),
            pltpu.VMEM(wide, jnp.float32),
            pltpu.VMEM(wide, jnp.float32),
            pltpu.VMEM(wide, jnp.float32),
            pltpu.VMEM((2, 2 * beam_count, dish_total), jnp.bfloat16),
            pltpu.SemaphoreType.DMA((4,)),
        ],
        name="solve",
    )(own, chan_index, loading, received, delay_rows)


def local(samples, delays, loading, chan_index, dish_map, steer_index):
    dish_count = lax.axis_size("dish")
    chan_count = lax.axis_size("chan")
    own = (lax.axis_index("dish") * chan_count + lax.axis_index("chan")).reshape(1)
    spectra = spectra_call(samples, chan_index)
    received = lax.all_to_all(spectra, ("dish", "chan"), 0, 0, tiled=True)
    received = received.reshape((dish_count, chan_count) + received.shape[1:])
    delay_rows = jnp.take(jnp.take(delays, steer_index, axis=0), dish_map, axis=1).T
    beams = solve_call(samples.shape[2], own, chan_index, loading, received, delay_rows)
    return lax.all_to_all(beams, "chan", 0, 0, tiled=True).astype(jnp.float32)


def solution(mesh):
    return jax.shard_map(
        local,
        mesh=mesh,
        in_specs=(P("chan", "dish", None), P(), P(), P(), P(), P()),
        out_specs=P("dish", None, "chan", None),
        check_vma=False,
    )
```

time: 113 us -> 105 us (0.929)
  Pallas kernels: 33.1 us -> 25.1 us
    pallas_call x1, Pallas kernels: 19.2 us -> 15.1 us  [solve_call(): pl.pallas_call(functools.partial(solve_kernel, sample_count), out_shape=j...]
    pallas_call x1, Pallas kernels: 13.8 us -> 9.97 us  [spectra_call(): pl.pallas_call(spectra_kernel, out_shape=jax.ShapeDtypeStruct((selected,...]
  transfers between devices with their start and end apart: 1 -> 1, of which waited for: 1 -> 1; matrix products, arithmetic and copies ran while one was open for 4% -> 5% of each run, Pallas kernels for 0% -> 0%
where the time goes in v2:
time: 105 us
  waiting for transfers between devices  48.2 us (46%)
  Pallas kernels  25.1 us (24%)
  blocking collectives  13.4 us (13%)
  starting transfers between devices  11.9 us (11%)
  local copies, waits for them, and re-layouts  3.82 us (4%)
  other arithmetic  2.2 us (2%)
    all_to_all x1, waiting for transfers between devices, local(): received = lax.all_to_all(spectra, ('dish', 'chan'), 0, 0, tiled=True)  48.2 us
    pallas_call x1, Pallas kernels, solve_call(): pl.pallas_call(functools.partial(solve_kernel, sample_count), out_shape=j...  15.1 us
    all_to_all x1, blocking collectives, local(): return lax.all_to_all(beams, 'chan', 0, 0, tiled=True).astype(jnp.float32)  13.4 us
    all_to_all x1, starting transfers between devices, local(): received = lax.all_to_all(spectra, ('dish', 'chan'), 0, 0, tiled=True)  11.9 us
    pallas_call x1, Pallas kernels, spectra_call(): pl.pallas_call(spectra_kernel, out_shape=jax.ShapeDtypeStruct((selected,...  9.97 us
    gather x1, local copies, waits for them, and re-layouts, local(): jnp.take(jnp.take(delays, steer_index, axis=0), dish_map, axis=1)  2.81 us
  transfers between devices with their start and end apart: 1, of which 1 were waited for; matrix products, arithmetic and copies ran while one was open for 5% of the time, Pallas kernels for 0%

profile of v2, /device:TPU:0, one launch (start us, length us, event | category | flops | bytes accessed | tf_op | source)
XLA Modules:
  0.0 104.7 jit_solution(16939324062201808792)
XLA Ops:
  0.0 0.0 copy-start
  0.0 10.0 %spectra.1 = bf16[128,2,64,128]{3,2,1,0:T(8,128)(2,1)} custom-call(s32[1,128]{1,0:T(1,128)} %bitcast.5, bf16[2,64,64,1024]{3,2,1,0:T(8,128)(2,1)} %bitcast.4), custom_call_target="tpu_custom_call" | custom-call | tf_op jit(solution)/shard_map/spectra/pallas_call | solution.py:125
  10.0 0.0 copy-start.2
  10.0 11.9 %all-to-all-start = ((bf16[128,2,64,128]{3,2,1,0:T(8,128)(2,1)}), bf16[128,2,64,128]{3,2,1,0:T(8,128)(2,1)}, u32[]{:S(2)}, u32[]{:S(2)}) async-start(bf16[128,2,64,128]{3,2,1,0:T(8,128)(2,1)} %spectra.1), calls=%async_computation | async-start | bytes 8388608 | tf_op jit(solution)/shard_map/all_to_all | solution.py:338
  21.9 0.0 copy-start.1
  21.9 0.0 copy-done.2
  21.9 0.0 copy-done
  22.0 0.8 gather_fusion
  22.8 0.1 broadcast_select_fusion.1
  22.9 0.2 copy.7
  23.1 0.0 copy-done.1
  23.1 2.8 %gather_fusion.1 = f32[1024,128]{1,0:T(8,128)S(1)} fusion(f32[128,1024]{0,1:T(8,128)S(1)} %copy.7, s32[1024]{0:T(1024)S(1)} %fusion), kind=kCustom, calls=%fused_computation.1 | custom fusion | bytes 1052672 | tf_op jit(solution)/shard_map/jit(_take)/gather | solution.py:340
  25.9 1.0 broadcast_select_fusion.delay_ref
  26.9 48.2 %all-to-all-done = bf16[128,2,64,128]{3,2,1,0:T(8,128)(2,1)} async-done(((bf16[128,2,64,128]{3,2,1,0:T(8,128)(2,1)}), bf16[128,2,64,128]{3,2,1,0:T(8,128)(2,1)}, u32[]{:S(2)}, u32[]{:S(2)}) %all-to-all-start) | async-done | bytes 4194336 | tf_op jit(solution)/shard_map/all_to_all | solution.py:338
  75.1 15.1 %solve.1 = bf16[8,2,128,128]{3,2,1,0:T(8,128)(2,1)} custom-call(s32[1]{0:T(128)} %bitcast.own_ref, s32[128]{0:T(128)} %chan_ref.1, f32[128]{0:T(128)} %load_ref.1, bf16[16,8,2,64,128]{4,3,2,1,0:T(8,128)(2,1)} %bitcast.3.recv_ref, f32[1024,128]{1,0:T(8,128)} %broadcast_select_fusion.delay_ref), custom_call_target="tpu_custom_call" | custom-call | tf_op jit(solution)/shard_map/solve/pallas_call | solution.py:311
  90.2 13.4 %all_to_all.10 = bf16[8,2,128,128]{3,2,1,0:T(8,128)(2,1)S(1)} all-to-all(bf16[8,2,128,128]{3,2,1,0:T(8,128)(2,1)} %solve.1), channel_id=1, replica_groups=mesh['dish'=16,'chan'=8] {'chan'}, dimensions={0} | all-to-all | bytes 1048576 | tf_op jit(solution)/shard_map/all_to_all | solution.py:342
  103.7 1.1 %convert_element_type.3 = f32[8,2,128,128]{3,2,1,0:T(8,128)} convert(bf16[8,2,128,128]{3,2,1,0:T(8,128)(2,1)S(1)} %all_to_all.10) | non-fusion elementwise | flops 262144 | bytes 1572864 | tf_op jit(solution)/shard_map/convert_element_type | solution.py:342
  (5 shorter events, 0.0 us)
Async XLA Ops:
  0.0 22.0 %copy-start = (f32[512,1024]{1,0:T(8,128)S(1)}, f32[512,1024]{1,0:T(8,128)}, u32[]{:S(2)}) copy-start(f32[512,1024]{1,0:T(8,128)} %param.7) | copy-start | bytes 6291460
  10.0 11.9 %copy-start.2 = (s32[128]{0:T(128)S(1)}, s32[128]{0:T(128)}, u32[]{:S(2)}) copy-start(s32[128]{0:T(128)} %param.11) | copy-start | bytes 1540
  10.0 65.1 %all-to-all-start = ((bf16[128,2,64,128]{3,2,1,0:T(8,128)(2,1)}), bf16[128,2,64,128]{3,2,1,0:T(8,128)(2,1)}, u32[]{:S(2)}, u32[]{:S(2)}) async-start(bf16[128,2,64,128]{3,2,1,0:T(8,128)(2,1)} %spectra.1), calls=%async_computation | async-start | bytes 8388608 | tf_op jit(solution)/shard_map/all_to_all | solution.py:338
  21.9 1.2 %copy-start.1 = (s32[1024]{0:T(1024)S(1)}, s32[1024]{0:T(1024)}, u32[]{:S(2)}) copy-start(s32[1024]{0:T(1024)} %param.10) | copy-start | bytes 12292

commit v3 on v2

--- a/solution.py
+++ b/solution.py
@@ -149,7 +149,9 @@
     out_ref,
     held_ref,
     joined_ref,
-    turned_ref,
+    sum_ref,
+    diff_ref,
+    cross_ref,
     real_ref,
     imag_ref,
     packed_ref,
@@ -185,14 +187,18 @@
         if block % each == 0:
             loads[block // each].wait()
         rows = slice(block * dish_local, (block + 1) * dish_local)
-        for part in range(2):
-            flipped = held_ref[block, :, part].reshape(span, LANES).T
-            for side in range(2):
-                values = flipped[side * dish_local : (side + 1) * dish_local, :]
-                first = part * frames + side * span
-                joined_ref[rows, first : first + span] = values
-                other = (1 - part) * frames + side * span
-                turned_ref[rows, other : other + span] = values if part == 1 else -values
+        real_part, imag_part = (
+            held_ref[block, :, part].reshape(span, LANES).T for part in range(2)
+        )
+        for side in range(2):
+            inner = slice(side * dish_local, (side + 1) * dish_local)
+            cols = slice(side * span, (side + 1) * span)
+            joined_ref[rows, side * span : (side + 1) * span] = real_part[inner, :]
+            joined_ref[rows, frames + side * span : frames + (side + 1) * span] = imag_part[
+                inner, :
+            ]
+            sum_ref[rows, cols] = real_part[inner, :] + imag_part[inner, :]
+            diff_ref[rows, cols] = real_part[inner, :] - imag_part[inner, :]
 
     tiles = [slice(first, first + TILE) for first in range(0, dish_total, TILE)]
     same = lax.broadcasted_iota(jnp.int32, (TILE, TILE), 0) == lax.broadcasted_iota(
@@ -201,26 +207,35 @@
     trace = jnp.zeros((1, TILE), jnp.float32)
     energy = jnp.zeros((1, TILE), jnp.float32)
     for index, cols in enumerate(tiles):
-        right = joined_ref[cols, :]
         top = cols.stop
-        cov_real = lax.dot_general(
-            joined_ref[0:top, :], right, NT, preferred_element_type=jnp.float32
-        )
-        cov_imag = lax.dot_general(
-            turned_ref[0:top, :], right, NT, preferred_element_type=jnp.float32
-        )
-        square = cov_real * cov_real + cov_imag * cov_imag
-        trace = trace + jnp.sum(jnp.where(same, cov_real[cols, :], 0.0), axis=0, keepdims=True)
-        energy = energy + jnp.sum(square[cols, :], axis=0, keepdims=True)
-        packed_real = cov_real.astype(jnp.bfloat16)
-        packed_imag = cov_imag.astype(jnp.bfloat16)
-        real_ref[0:top, cols] = packed_real
-        imag_ref[0:top, cols] = packed_imag
-        if index:
-            energy = energy + 2.0 * jnp.sum(square[0 : cols.start, :], axis=0, keepdims=True)
-        for rows in tiles[:index]:
-            real_ref[cols, rows] = packed_real[rows, :].T
-            imag_ref[cols, rows] = -packed_imag[rows, :].T
+        cross_ref[:, cols] = lax.dot_general(
+            sum_ref[...], diff_ref[cols, :], NT, preferred_element_type=jnp.float32
+        )
+        square_imag = lax.dot_general(
+            joined_ref[0:top, frames:],
+            joined_ref[cols, frames:],
+            NT,
+            preferred_element_type=jnp.float32,
+        )
+        for rows in tiles[: index + 1]:
+            upper_part = cross_ref[rows, cols]
+            lower_part = cross_ref[cols, rows].T
+            cov_real = 0.5 * (upper_part + lower_part) + 2.0 * square_imag[rows, :]
+            cov_imag = 0.5 * (upper_part - lower_part)
+            square = cov_real * cov_real + cov_imag * cov_imag
+            share = jnp.sum(square, axis=0, keepdims=True)
+            packed_real = cov_real.astype(jnp.bfloat16)
+            packed_imag = cov_imag.astype(jnp.bfloat16)
+            real_ref[rows, cols] = packed_real
+            imag_ref[rows, cols] = packed_imag
+            if rows == cols:
+                diagonal = jnp.where(same, cov_real, 0.0)
+                trace = trace + jnp.sum(diagonal, axis=0, keepdims=True)
+                energy = energy + share
+            else:
+                energy = energy + 2.0 * share
+                real_ref[cols, rows] = packed_real.T
+                imag_ref[cols, rows] = -packed_imag.T
 
     def full(value):
         return jnp.full((1, 2 * beam_count), value, jnp.float32)
@@ -316,7 +331,9 @@
         scratch_shapes=[
             pltpu.VMEM(received.shape, jnp.bfloat16),
             pltpu.VMEM((dish_total, 2 * frames), jnp.bfloat16),
-            pltpu.VMEM((dish_total, 2 * frames), jnp.bfloat16),
+            pltpu.VMEM((dish_total, frames), jnp.bfloat16),
+            pltpu.VMEM((dish_total, frames), jnp.bfloat16),
+            pltpu.VMEM((dish_total, dish_total), jnp.float32),
             pltpu.VMEM((dish_total, dish_total), jnp.bfloat16),
             pltpu.VMEM((dish_total, dish_total), jnp.bfloat16),
             pltpu.VMEM((2,) + wide, jnp.bfloat16),

time: 105 us -> 103 us (0.981)
  Pallas kernels: 25.1 us -> 23.4 us
    pallas_call x1, Pallas kernels: 15.1 us -> 13.5 us  [solve_call(): pl.pallas_call(functools.partial(solve_kernel, sample_count), out_shape=j...]
where the time goes in v3:
time: 103 us
  waiting for transfers between devices  48.2 us (47%)
  Pallas kernels  23.4 us (23%)
  blocking collectives  13.4 us (13%)
  starting transfers between devices  11.9 us (12%)
  local copies, waits for them, and re-layouts  3.82 us (4%)
  other arithmetic  2.2 us (2%)
    all_to_all x1, waiting for transfers between devices, local(): received = lax.all_to_all(spectra, ('dish', 'chan'), 0, 0, tiled=True)  48.2 us
    pallas_call x1, Pallas kernels, solve_call(): pl.pallas_call(functools.partial(solve_kernel, sample_count), out_shape=j...  13.5 us
    all_to_all x1, blocking collectives, local(): return lax.all_to_all(beams, 'chan', 0, 0, tiled=True).astype(jnp.float32)  13.4 us
    all_to_all x1, starting transfers between devices, local(): received = lax.all_to_all(spectra, ('dish', 'chan'), 0, 0, tiled=True)  11.9 us
    pallas_call x1, Pallas kernels, spectra_call(): pl.pallas_call(spectra_kernel, out_shape=jax.ShapeDtypeStruct((selected,...  9.97 us
    gather x1, local copies, waits for them, and re-layouts, local(): jnp.take(jnp.take(delays, steer_index, axis=0), dish_map, axis=1)  2.81 us
  transfers between devices with their start and end apart: 1, of which 1 were waited for; matrix products, arithmetic and copies ran while one was open for 5% of the time, Pallas kernels for 0%

profile of v3, /device:TPU:0, one launch (start us, length us, event | category | flops | bytes accessed | tf_op | source)
XLA Modules:
  0.0 103.1 jit_solution(17188656381362251464)
XLA Ops:
  0.0 0.0 copy-start
  0.0 10.0 %spectra.1 = bf16[128,2,64,128]{3,2,1,0:T(8,128)(2,1)} custom-call(s32[1,128]{1,0:T(1,128)} %bitcast.5, bf16[2,64,64,1024]{3,2,1,0:T(8,128)(2,1)} %bitcast.4), custom_call_target="tpu_custom_call" | custom-call | tf_op jit(solution)/shard_map/spectra/pallas_call | solution.py:125
  10.0 0.0 copy-start.2
  10.0 11.9 %all-to-all-start = ((bf16[128,2,64,128]{3,2,1,0:T(8,128)(2,1)}), bf16[128,2,64,128]{3,2,1,0:T(8,128)(2,1)}, u32[]{:S(2)}, u32[]{:S(2)}) async-start(bf16[128,2,64,128]{3,2,1,0:T(8,128)(2,1)} %spectra.1), calls=%async_computation | async-start | bytes 8388608 | tf_op jit(solution)/shard_map/all_to_all | solution.py:355
  21.9 0.0 copy-start.1
  21.9 0.0 copy-done.2
  21.9 0.0 copy-done
  22.0 0.8 gather_fusion
  22.8 0.1 broadcast_select_fusion.1
  22.9 0.2 copy.7
  23.1 0.0 copy-done.1
  23.1 2.8 %gather_fusion.1 = f32[1024,128]{1,0:T(8,128)S(1)} fusion(f32[128,1024]{0,1:T(8,128)S(1)} %copy.7, s32[1024]{0:T(1024)S(1)} %fusion), kind=kCustom, calls=%fused_computation.1 | custom fusion | bytes 1052672 | tf_op jit(solution)/shard_map/jit(_take)/gather | solution.py:357
  25.9 1.0 broadcast_select_fusion.delay_ref
  26.9 48.2 %all-to-all-done = bf16[128,2,64,128]{3,2,1,0:T(8,128)(2,1)} async-done(((bf16[128,2,64,128]{3,2,1,0:T(8,128)(2,1)}), bf16[128,2,64,128]{3,2,1,0:T(8,128)(2,1)}, u32[]{:S(2)}, u32[]{:S(2)}) %all-to-all-start) | async-done | bytes 4194336 | tf_op jit(solution)/shard_map/all_to_all | solution.py:355
  75.1 13.5 %solve.1 = bf16[8,2,128,128]{3,2,1,0:T(8,128)(2,1)} custom-call(s32[1]{0:T(128)} %bitcast.own_ref, s32[128]{0:T(128)} %chan_ref.1, f32[128]{0:T(128)} %load_ref.1, bf16[16,8,2,64,128]{4,3,2,1,0:T(8,128)(2,1)} %bitcast.3.recv_ref, f32[1024,128]{1,0:T(8,128)} %broadcast_select_fusion.delay_ref), custom_call_target="tpu_custom_call" | custom-call | tf_op jit(solution)/shard_map/solve/pallas_call | solution.py:326
  88.6 13.4 %all_to_all.10 = bf16[8,2,128,128]{3,2,1,0:T(8,128)(2,1)S(1)} all-to-all(bf16[8,2,128,128]{3,2,1,0:T(8,128)(2,1)} %solve.1), channel_id=1, replica_groups=mesh['dish'=16,'chan'=8] {'chan'}, dimensions={0} | all-to-all | bytes 1048576 | tf_op jit(solution)/shard_map/all_to_all | solution.py:359
  102.0 1.1 %convert_element_type.3 = f32[8,2,128,128]{3,2,1,0:T(8,128)} convert(bf16[8,2,128,128]{3,2,1,0:T(8,128)(2,1)S(1)} %all_to_all.10) | non-fusion elementwise | flops 262144 | bytes 1572864 | tf_op jit(solution)/shard_map/convert_element_type | solution.py:359
  (5 shorter events, 0.0 us)
Async XLA Ops:
  0.0 22.0 %copy-start = (f32[512,1024]{1,0:T(8,128)S(1)}, f32[512,1024]{1,0:T(8,128)}, u32[]{:S(2)}) copy-start(f32[512,1024]{1,0:T(8,128)} %param.7) | copy-start | bytes 6291460
  10.0 11.9 %copy-start.2 = (s32[128]{0:T(128)S(1)}, s32[128]{0:T(128)}, u32[]{:S(2)}) copy-start(s32[128]{0:T(128)} %param.11) | copy-start | bytes 1540
  10.0 65.1 %all-to-all-start = ((bf16[128,2,64,128]{3,2,1,0:T(8,128)(2,1)}), bf16[128,2,64,128]{3,2,1,0:T(8,128)(2,1)}, u32[]{:S(2)}, u32[]{:S(2)}) async-start(bf16[128,2,64,128]{3,2,1,0:T(8,128)(2,1)} %spectra.1), calls=%async_computation | async-start | bytes 8388608 | tf_op jit(solution)/shard_map/all_to_all | solution.py:355
  21.9 1.2 %copy-start.1 = (s32[1024]{0:T(1024)S(1)}, s32[1024]{0:T(1024)}, u32[]{:S(2)}) copy-start(s32[1024]{0:T(1024)} %param.10) | copy-start | bytes 12292

commit v4 on v3

--- a/solution.py
+++ b/solution.py
@@ -1,4 +1,3 @@
-import functools
 import math
 
 import jax
@@ -140,12 +139,10 @@
 
 
 def solve_kernel(
-    sample_count,
     own_ref,
-    chan_ref,
     load_ref,
     recv_ref,
-    delay_ref,
+    steer_ref,
     out_ref,
     held_ref,
     joined_ref,
@@ -160,15 +157,15 @@
     dir_ref,
     weight_ref,
     sems,
+    steer_sem,
 ):
     blocks, groups, _, half, _ = recv_ref.shape
-    dish_total, beam_count = delay_ref.shape
+    dish_total, beam_count = steer_ref.shape[0], steer_ref.shape[1] // 2
     dish_local = dish_total // blocks
     span = groups * half
     frames = 2 * span
     own = own_ref[0]
     delta = load_ref[own]
-    bin_number = chan_ref[own].astype(jnp.float32)
     on_real, on_imag = slice(0, beam_count), slice(beam_count, 2 * beam_count)
 
     loads = []
@@ -177,11 +174,6 @@
         part = slice(index * each, (index + 1) * each)
         loads.append(pltpu.make_async_copy(recv_ref.at[part], held_ref.at[part], sems.at[index]))
         loads[-1].start()
-
-    turns = bin_number * delay_ref[...] * (-1.0 / sample_count)
-    steer_real, steer_imag = sincos_turns(turns - jnp.round(turns))
-    res_ref[:, on_real] = steer_real
-    res_ref[:, on_imag] = steer_imag
 
     for block in range(blocks):
         if block % each == 0:
@@ -199,6 +191,9 @@
             ]
             sum_ref[rows, cols] = real_part[inner, :] + imag_part[inner, :]
             diff_ref[rows, cols] = real_part[inner, :] - imag_part[inner, :]
+
+    steer_load = pltpu.make_async_copy(steer_ref, res_ref, steer_sem)
+    steer_load.start()
 
     tiles = [slice(first, first + TILE) for first in range(0, dish_total, TILE)]
     same = lax.broadcasted_iota(jnp.int32, (TILE, TILE), 0) == lax.broadcasted_iota(
@@ -236,6 +231,8 @@
                 energy = energy + 2.0 * share
                 real_ref[cols, rows] = packed_real.T
                 imag_ref[cols, rows] = -packed_imag.T
+
+    steer_load.wait()
 
     def full(value):
         return jnp.full((1, 2 * beam_count), value, jnp.float32)
@@ -315,18 +312,18 @@
                     )
 
 
-def solve_call(sample_count, own, chan_index, loading, received, delay_rows):
+def solve_call(own, loading, received, steering):
     blocks, groups, _, half, _ = received.shape
-    dish_total, beam_count = delay_rows.shape
+    dish_total, beam_count = steering.shape[0], steering.shape[1] // 2
     frames = 2 * groups * half
     smem = pl.BlockSpec(memory_space=pltpu.SMEM)
     vmem = pl.BlockSpec(memory_space=pltpu.VMEM)
     hbm = pl.BlockSpec(memory_space=pl.ANY)
     wide = (dish_total, 2 * beam_count)
     return pl.pallas_call(
-        functools.partial(solve_kernel, sample_count),
+        solve_kernel,
         out_shape=jax.ShapeDtypeStruct((groups, 2, 2 * half, beam_count), jnp.bfloat16),
-        in_specs=[smem, smem, smem, hbm, vmem],
+        in_specs=[smem, smem, hbm, hbm],
         out_specs=vmem,
         scratch_shapes=[
             pltpu.VMEM(received.shape, jnp.bfloat16),
@@ -342,9 +339,10 @@
             pltpu.VMEM(wide, jnp.float32),
             pltpu.VMEM((2, 2 * beam_count, dish_total), jnp.bfloat16),
             pltpu.SemaphoreType.DMA((4,)),
+            pltpu.SemaphoreType.DMA(()),
         ],
         name="solve",
-    )(own, chan_index, loading, received, delay_rows)
+    )(own, loading, received, steering)
 
 
 def local(samples, delays, loading, chan_index, dish_map, steer_index):
@@ -355,7 +353,10 @@
     received = lax.all_to_all(spectra, ("dish", "chan"), 0, 0, tiled=True)
     received = received.reshape((dish_count, chan_count) + received.shape[1:])
     delay_rows = jnp.take(jnp.take(delays, steer_index, axis=0), dish_map, axis=1).T
-    beams = solve_call(samples.shape[2], own, chan_index, loading, received, delay_rows)
+    bin_number = lax.dynamic_index_in_dim(chan_index, own[0], 0, False).astype(jnp.float32)
+    turns = bin_number * delay_rows * (-1.0 / samples.shape[2])
+    steering = jnp.concatenate(sincos_turns(turns - jnp.round(turns)), axis=1)
+    beams = solve_call(own, loading, received, steering)
     return lax.all_to_all(beams, "chan", 0, 0, tiled=True).astype(jnp.float32)
 
 

time: 103 us -> 103 us (level)
  waiting for transfers between devices: 48.2 us -> 46 us
    all_to_all x1, waiting for transfers between devices: 48.2 us -> 46 us  [local(): received = lax.all_to_all(spectra, ('dish', 'chan'), 0, 0, tiled=True)]
    concatenate x0 -> x1, other arithmetic: none -> 1.04 us  [local(): steering = jnp.concatenate(sincos_turns(turns - jnp.round(turns)), axis=1)]
  transfers between devices with their start and end apart: 1 -> 1, of which waited for: 1 -> 1; matrix products, arithmetic and copies ran while one was open for 5% -> 6% of each run, Pallas kernels for 0% -> 0%
where the time goes in v4:
time: 103 us
  waiting for transfers between devices  46 us (45%)
  Pallas kernels  22.9 us (22%)
  blocking collectives  13.4 us (13%)
  starting transfers between devices  11.9 us (12%)
  local copies, waits for them, and re-layouts  4.41 us (4%)
  other arithmetic  3.07 us (3%)
    all_to_all x1, waiting for transfers between devices, local(): received = lax.all_to_all(spectra, ('dish', 'chan'), 0, 0, tiled=True)  46 us
    all_to_all x1, blocking collectives, local(): return lax.all_to_all(beams, 'chan', 0, 0, tiled=True).astype(jnp.float32)  13.4 us
    pallas_call x1, Pallas kernels, solve_call(): pl.pallas_call(solve_kernel, out_shape=jax.ShapeDtypeStruct((groups, 2, 2...  13 us
    all_to_all x1, starting transfers between devices, local(): received = lax.all_to_all(spectra, ('dish', 'chan'), 0, 0, tiled=True)  11.9 us
    pallas_call x1, Pallas kernels, spectra_call(): pl.pallas_call(spectra_kernel, out_shape=jax.ShapeDtypeStruct((selected,...  9.96 us
    gather x1, local copies, waits for them, and re-layouts, local(): jnp.take(jnp.take(delays, steer_index, axis=0), dish_map, axis=1)  2.81 us
  transfers between devices with their start and end apart: 1, of which 1 were waited for; matrix products, arithmetic and copies ran while one was open for 6% of the time, Pallas kernels for 0%

profile of v4, /device:TPU:0, one launch (start us, length us, event | category | flops | bytes accessed | tf_op | source)
XLA Modules:
  0.0 102.6 jit_solution(18255466590407902895)
XLA Ops:
  0.0 0.0 copy-start
  0.0 10.0 %spectra.1 = bf16[128,2,64,128]{3,2,1,0:T(8,128)(2,1)} custom-call(s32[1,128]{1,0:T(1,128)} %bitcast.6, bf16[2,64,64,1024]{3,2,1,0:T(8,128)(2,1)} %bitcast.5), custom_call_target="tpu_custom_call" | custom-call | tf_op jit(solution)/shard_map/spectra/pallas_call | solution.py:124
  10.0 0.0 copy-start.3
  10.0 11.9 %all-to-all-start = ((bf16[128,2,64,128]{3,2,1,0:T(8,128)(2,1)}), bf16[128,2,64,128]{3,2,1,0:T(8,128)(2,1)}, u32[]{:S(2)}, u32[]{:S(2)}) async-start(bf16[128,2,64,128]{3,2,1,0:T(8,128)(2,1)} %spectra.1), calls=%async_computation | async-start | bytes 8388608 | tf_op jit(solution)/shard_map/all_to_all | solution.py:353
  21.9 0.0 copy-start.2
  21.9 0.0 copy-start.1
  21.9 0.0 copy-done.3
  22.0 0.0 copy-done
  22.0 0.8 gather_fusion
  22.8 0.1 broadcast_select_fusion
  22.9 0.2 copy.7
  23.1 0.0 copy-done.2
  23.1 0.6 dynamic_slice.4
  24.4 0.0 copy-done.1
  24.4 2.8 %gather_fusion.1 = f32[1024,128]{1,0:T(8,128)S(1)} fusion(f32[128,1024]{0,1:T(8,128)S(1)} %copy.7, s32[1024]{0:T(1024)S(1)} %fusion.2), kind=kCustom, calls=%fused_computation.1 | custom fusion | bytes 1052672 | tf_op jit(solution)/shard_map/jit(_take)/gather | solution.py:355
  27.2 0.8 negate_select_fusion.1
  28.0 1.0 %pad_maximum_fusion.steer_ref = f32[1024,256]{1,0:T(8,128)} fusion(f32[1024,128]{1,0:T(8,128)S(1)} %get-tuple-element.6, f32[1024,128]{1,0:T(8,128)S(1)} %get-tuple-element.5), kind=kLoop, calls=%fused_computation.2 | loop fusion | flops 262144 | bytes 2097152 | tf_op jit(solution)/shard_map/concatenate | solution.py:358
  29.1 46.0 %all-to-all-done = bf16[128,2,64,128]{3,2,1,0:T(8,128)(2,1)} async-done(((bf16[128,2,64,128]{3,2,1,0:T(8,128)(2,1)}), bf16[128,2,64,128]{3,2,1,0:T(8,128)(2,1)}, u32[]{:S(2)}, u32[]{:S(2)}) %all-to-all-start) | async-done | bytes 4194336 | tf_op jit(solution)/shard_map/all_to_all | solution.py:353
  75.1 13.0 %solve.1 = bf16[8,2,128,128]{3,2,1,0:T(8,128)(2,1)} custom-call(s32[1]{0:T(128)} %bitcast.own_ref, f32[128]{0:T(128)} %load_ref.1, bf16[16,8,2,64,128]{4,3,2,1,0:T(8,128)(2,1)} %bitcast.3.recv_ref, f32[1024,256]{1,0:T(8,128)} %pad_maximum_fusion.steer_ref), custom_call_target="tpu_custom_call" | custom-call | tf_op jit(solution)/shard_map/solve/pallas_call | solution.py:323
  88.1 13.4 %all_to_all.10 = bf16[8,2,128,128]{3,2,1,0:T(8,128)(2,1)S(1)} all-to-all(bf16[8,2,128,128]{3,2,1,0:T(8,128)(2,1)} %solve.1), channel_id=1, replica_groups=mesh['dish'=16,'chan'=8] {'chan'}, dimensions={0} | all-to-all | bytes 1048576 | tf_op jit(solution)/shard_map/all_to_all | solution.py:360
  101.5 1.1 %convert_element_type.15 = f32[8,2,128,128]{3,2,1,0:T(8,128)} convert(bf16[8,2,128,128]{3,2,1,0:T(8,128)(2,1)S(1)} %all_to_all.10) | non-fusion elementwise | flops 262144 | bytes 1572864 | tf_op jit(solution)/shard_map/convert_element_type | solution.py:360
  (5 shorter events, 0.0 us)
Async XLA Ops:
  0.0 22.0 %copy-start = (f32[512,1024]{1,0:T(8,128)S(1)}, f32[512,1024]{1,0:T(8,128)}, u32[]{:S(2)}) copy-start(f32[512,1024]{1,0:T(8,128)} %param.7) | copy-start | bytes 6291460
  10.0 11.9 %copy-start.3 = (s32[128]{0:T(128)S(1)}, s32[128]{0:T(128)}, u32[]{:S(2)}) copy-start(s32[128]{0:T(128)} %param.11) | copy-start | bytes 1540
  10.0 65.1 %all-to-all-start = ((bf16[128,2,64,128]{3,2,1,0:T(8,128)(2,1)}), bf16[128,2,64,128]{3,2,1,0:T(8,128)(2,1)}, u32[]{:S(2)}, u32[]{:S(2)}) async-start(bf16[128,2,64,128]{3,2,1,0:T(8,128)(2,1)} %spectra.1), calls=%async_computation | async-start | bytes 8388608 | tf_op jit(solution)/shard_map/all_to_all | solution.py:353
  21.9 1.2 %copy-start.2 = (s32[128]{0:T(128)S(1)}, s32[128]{0:T(128)}, u32[]{:S(2)}) copy-start(s32[128]{0:T(128)} %param.9) | copy-start | bytes 1540
  21.9 2.4 %copy-start.1 = (s32[1024]{0:T(1024)S(1)}, s32[1024]{0:T(1024)}, u32[]{:S(2)}) copy-start(s32[1024]{0:T(1024)} %param.10) | copy-start | bytes 12292
